TPU v7x, 128 devices: a whole 4x4x4 slice. The times are simulated.
128 devices in a mesh: req: 16 (over x, z), mlp: 8 (over y, core).
Axes of the slice: x: 4, y: 4, z: 4, core: 2. Of those that a mesh axis runs over, the one named last changes fastest.
Arguments:
- patches: bfloat16 [15360, 4096], P('req'), may hold values from -6 to 6
- norm_gain: float32 [4096], replicated, may hold values from 0.25 to 1.75
- norm_bias: float32 [4096], replicated, may hold values from -3 to 3
- gate_weight: bfloat16 [4096, 8192], P(None, ('req', 'mlp')), may hold values from -0.09375 to 0.09375
- up_weight: bfloat16 [4096, 8192], P(None, ('req', 'mlp')), may hold values from -0.09375 to 0.09375
- down_weight: bfloat16 [4096, 8192], P(None, ('req', 'mlp')), may hold values from -0.0625 to 0.0625
- layer_scale: float32 [4096], replicated, may hold values from 0.25 to 2.5
- projection: bfloat16 [4, 4096, 4096], P(None, 'mlp', 'req'), may hold values from -0.046875 to 0.046875
- text_rows: bfloat16 [65536, 4096], P(('req', 'mlp')), may hold values from -6 to 6
- destination: int32 [3840], replicated, may hold values from -1 to 65535, as said below
Outputs:
- patch_out: bfloat16 [15360, 4096], P('req', 'mlp')
- streams: bfloat16 [65536, 4096], P(('req', 'mlp'))
Inputs may be any that keep to these rules, and one draw needn't show every extreme that they name: `destination`: values other than -1 are distinct positions; the positions landing in one piece of 512 consecutive positions (a stream holds 8 pieces) form one run of consecutive positions, at least one and at most 30 of them, and some piece receives exactly 30.
All inputs are finite; a program needn't handle non-finite values.
Results may differ from a plain program's by a relative error of at most 0.015.
Values may be sent and summed in bfloat16 or wider, within the bound.
No kernel may reach another device: no remote copies, remote signals or barrier semaphores. Data moves between devices by JAX's collectives and lax.ppermute only.
A program may use at most 128 MiB of HBM per device.

v0:
```python
import jax
import jax.numpy as jnp
from jax import lax
from jax.sharding import PartitionSpec as P


def layer_norm(values, norm_gain, norm_bias):
    row_mean = jnp.mean(values, axis=-1, keepdims=True)
    centred = values - row_mean
    variance = jnp.mean(centred * centred, axis=-1, keepdims=True)
    return centred * lax.rsqrt(variance + 1e-06) * norm_gain + norm_bias


def shards(
    patches,
    norm_gain,
    norm_bias,
    gate_weight,
    up_weight,
    down_weight,
    layer_scale,
    projection,
    text_rows,
    destination,
):
    req_count = lax.axis_size("req")
    mlp_count = lax.axis_size("mlp")
    req_index = lax.axis_index("req")
    mlp_index = lax.axis_index("mlp")
    rows_here, model_width = patches.shape
    feat_width = model_width // mlp_count
    inputs = patches.astype(jnp.float32)
    normed = layer_norm(inputs, norm_gain, norm_bias).astype(jnp.bfloat16)
    gate_act = jnp.dot(
        normed,
        lax.all_gather(gate_weight, "req", axis=1, tiled=True),
        preferred_element_type=jnp.float32,
    )
    up_act = jnp.dot(
        normed,
        lax.all_gather(up_weight, "req", axis=1, tiled=True),
        preferred_element_type=jnp.float32,
    )
    hidden = (jax.nn.silu(gate_act) * up_act).astype(jnp.bfloat16)
    ffn_local = lax.dot_general(
        hidden,
        lax.all_gather(down_weight, "req", axis=1, tiled=True),
        (((1,), (1,)), ((), ())),
        preferred_element_type=jnp.float32,
    )
    partial_value = lax.optimization_barrier(ffn_local.astype(jnp.bfloat16)).astype(jnp.float32)
    ffn_feats = lax.psum_scatter(
        partial_value.astype(jnp.bfloat16), "mlp", scatter_dimension=1, tiled=True
    ).astype(jnp.float32)
    scale_here = lax.dynamic_slice_in_dim(layer_scale, mlp_index * feat_width, feat_width)
    own_inputs = lax.dynamic_slice_in_dim(inputs, mlp_index * feat_width, feat_width, axis=1)
    patch_out = (own_inputs + scale_here * ffn_feats).astype(jnp.bfloat16)
    merged = patch_out.reshape(rows_here // 4, 4 * feat_width)
    weight_cols = projection.reshape(4 * feat_width, projection.shape[2])
    piece_rows = text_rows.shape[0]
    slot_count = destination.shape[0]
    bucket_count = req_count * mlp_count
    capacity = slot_count // bucket_count
    is_valid = destination >= 0
    piece_ids = jnp.where(is_valid, destination // piece_rows, -1)
    offsets = destination % piece_rows
    bucket_hit = piece_ids[:, None] == jnp.arange(bucket_count, dtype=jnp.int32)[None, :]
    first_off = jnp.min(jnp.where(bucket_hit, offsets[:, None], piece_rows), axis=0)
    counts = jnp.sum(bucket_hit.astype(jnp.int32), axis=0)
    slot_first = jnp.sum(jnp.where(bucket_hit, first_off[None, :], 0), axis=1)
    slot_rank = offsets - slot_first
    stream_ids = piece_ids // mlp_count
    piece_in = piece_ids % mlp_count
    rows_at = piece_in * (req_count * capacity) + stream_ids * capacity + slot_rank
    rows_at = jnp.where(is_valid, rows_at, bucket_count * capacity)
    sources = (
        jnp.full((bucket_count * capacity,), -1, jnp.int32)
        .at[rows_at]
        .set(jnp.arange(slot_count, dtype=jnp.int32), mode="drop")
    )
    every_row = lax.all_gather(merged, "req", axis=0, tiled=True)
    picked_rows = jnp.take(every_row, jnp.maximum(sources, 0), axis=0)
    picked_rows = jnp.where(sources[:, None] >= 0, picked_rows, jnp.zeros_like(picked_rows))
    summed = lax.psum_scatter(
        jnp.dot(picked_rows, weight_cols, preferred_element_type=jnp.float32).astype(jnp.bfloat16),
        "mlp",
        scatter_dimension=0,
        tiled=True,
    )
    arrived = lax.all_to_all(summed, "req", split_axis=0, concat_axis=1, tiled=True)
    bucket_here = req_index * mlp_count + mlp_index
    start_here = first_off[bucket_here]
    count_here = counts[bucket_here]
    positions = jnp.arange(piece_rows, dtype=jnp.int32) - start_here
    inside = (positions >= 0) & (positions < count_here)
    image_rows = jnp.take(arrived, jnp.clip(positions, 0, capacity - 1), axis=0)
    streams = jnp.where(inside[:, None], image_rows, text_rows)
    return (patch_out, streams)


def solution(mesh):
    return jax.shard_map(
        shards,
        mesh=mesh,
        in_specs=(
            P("req", None),
            P(),
            P(),
            P(None, ("req", "mlp")),
            P(None, ("req", "mlp")),
            P(None, ("req", "mlp")),
            P(),
            P(None, "mlp", "req"),
            P(("req", "mlp"), None),
            P(),
        ),
        out_specs=(P("req", "mlp"), P(("req", "mlp"), None)),
        check_vma=False,
    )
```

profile of v0, /device:TPU:0, one launch (start us, length us, event | category | flops | bytes accessed | tf_op | source)
XLA Modules:
  0.0 527.9 jit_solution(9855831558795438825)
XLA Ops:
  7.2 0.0 copy-start
  7.2 0.0 all-gather.5.cloned.1.call-start
  7.2 0.7 all-gather.5.cloned.1.call-update
  7.9 0.0 all-gather.7.cloned.1.call-start
  8.0 0.7 all-gather.7.cloned.1.call-update
  8.7 0.0 all-gather.9.cloned.1.call-start
  8.7 0.7 all-gather.9.cloned.1.call-update
  9.4 0.0 reduce-scatter.3.cloned.1.call-start
  9.4 0.0 copy-start.1
  9.5 0.0 copy-start.4
  9.5 0.0 copy-start.5
  9.5 4.5 convert_reduce_fusion
  14.0 1.0 copy-done.1
  14.9 2.2 multiply_reduce_fusion
  17.1 66.4 %all-gather.5.cloned.1.call-done = bf16[4096,1024]{0,1:T(8,128)(2,1)} async-done(((bf16[4096,64]{0,1:T(8,128)(2,1)}), bf16[4096,1024]{0,1:T(8,128)(2,1)}) %all-gather.5.cloned.1.call-update) | async-done | bytes 8388624 | tf_op jit(solution)/shard_map/all_gather | solution.py:36
  83.5 0.0 copy-done.4
  83.5 0.0 copy-done.5
  83.5 14.4 %fusion.31 = f32[960,1024]{1,0:T(8,128)} fusion(bf16[4096,1024]{0,1:T(8,128)(2,1)} %all-gather.5.cloned.1.call-done, bf16[960,4096]{1,0:T(8,128)(2,1)} %param.10, f32[4096]{0:T(1024)S(1)} %copy-done.4, f32[4096]{0:T(1024)S(1)} %copy-done.5, f32[960]{0:T(1024)S(1)} %add_rsqrt_fusion, f32[960]{0:T(1024)S(1)} %broadcast_multiply_fusion), kind=kOutput, calls=%fused_computation.68 | convolution fusion | flops 8076656640 | bytes 20225536 | tf_op jit(solution)/shard_map/dot_general | solution.py:34
  97.9 58.2 %all-gather.7.cloned.1.call-done = bf16[4096,1024]{0,1:T(8,128)(2,1)} async-done(((bf16[4096,64]{0,1:T(8,128)(2,1)}), bf16[4096,1024]{0,1:T(8,128)(2,1)}) %all-gather.7.cloned.1.call-update) | async-done | bytes 8388624 | tf_op jit(solution)/shard_map/all_gather | solution.py:41
  156.1 72.6 %all-gather.9.cloned.1.call-done = bf16[4096,1024]{0,1:T(8,128)(2,1)} async-done(((bf16[4096,64]{0,1:T(8,128)(2,1)}), bf16[4096,1024]{0,1:T(8,128)(2,1)}) %all-gather.9.cloned.1.call-update) | async-done | bytes 8388624 | tf_op jit(solution)/shard_map/all_gather | solution.py:47
  228.7 25.9 %convolution_convert_fusion = bf16[960,4096]{1,0:T(8,128)(2,1)} fusion(bf16[4096,1024]{0,1:T(8,128)(2,1)} %all-gather.9.cloned.1.call-done, f32[960,1024]{1,0:T(8,128)} %fusion.31, bf16[4096,1024]{0,1:T(8,128)(2,1)} %all-gather.7.cloned.1.call-done, bf16[960,4096]{1,0:T(8,128)(2,1)} %param.10, f32[4096]{0:T(1024)S(1)} %copy-done.4, f32[4096]{0:T(1024)S(1)} %copy-done.5, ...), kind=kOutput, calls=%fused_computation.13 | convolution fusion | flops 16139550720 | bytes 36478464 | tf_op jit(solution)/shard_map/dot_general | solution.py:45
  254.6 0.0 reduce-scatter.3.cloned.1.call-update
  254.6 0.0 all-gather.11.cloned.1.call-start
  254.7 0.0 copy-start.3
  254.7 11.3 %convert_element_type.26 = f32[960,4096]{1,0:T(8,128)} convert(bf16[960,4096]{1,0:T(8,128)(2,1)} %param.10) | non-fusion elementwise | flops 3932160 | bytes 23592960 | tf_op jit(solution)/shard_map/convert_element_type | solution.py:32
  266.0 0.8 dynamic_slice.13
  266.7 37.6 %reduce-scatter.3.cloned.1.call-done = bf16[960,512]{1,0:T(8,128)(2,1)} async-done(((bf16[960,4096]{1,0:T(8,128)(2,1)}), bf16[960,512]{1,0:T(8,128)(2,1)}) %reduce-scatter.3.cloned.1.call-update) | async-done | bytes 983056 | tf_op jit(solution)/shard_map/reduce_scatter | solution.py:52
  304.3 2.2 add_convert_fusion.1
  306.5 0.0 copy-start.2
  306.5 1.5 reshape.67
  308.0 0.0 all-gather.11.cloned.1.call-update
  308.0 0.0 reduce-scatter.5.cloned.1.call-start
  308.1 0.0 copy-done.3
  308.1 2.5 select_reduce_fusion.1
  310.6 2.4 convert_reduce_fusion.1
  313.1 14.6 %scatter_custom_fusion = s32[3840]{0:T(1024)S(1)} fusion(s32[3840]{0:T(1024)S(1)} %compare_select_fusion, s32[3840]{0:T(1024)S(1)} %iota.16, s32[]{:T(128)} %constant.104.clone.1), kind=kCustom, calls=%fused_computation.51 | custom fusion | bytes 15364 | tf_op jit(solution)/shard_map/scatter | solution.py:79
  327.7 86.2 %all-gather.11.cloned.1.call-done = bf16[3840,2048]{1,0:T(8,128)(2,1)} async-done(((bf16[240,2048]{1,0:T(8,128)(2,1)}), bf16[3840,2048]{1,0:T(8,128)(2,1)}) %all-gather.11.cloned.1.call-update) | async-done | bytes 15728656 | tf_op jit(solution)/shard_map/all_gather | solution.py:81
  413.9 37.0 %gather_fusion = bf16[3840,2048]{1,0:T(8,128)(2,1)} fusion(bf16[3840,2048]{1,0:T(8,128)(2,1)} %all-gather.11.cloned.1.call-done, s32[4096]{0:T(1024)S(1)} %pad_clamp_fusion), kind=kCustom, calls=%fused_computation | custom fusion | bytes 31472640 | tf_op jit(solution)/shard_map/jit(_take)/gather | solution.py:82
  450.9 0.0 copy-done.2
  450.9 0.0 copy-done
  450.9 9.9 %fusion.7 = bf16[3840,256]{1,0:T(8,128)(2,1)} fusion(bf16[2048,256]{1,0:T(8,128)(2,1)S(1)} %bitcast.13, bf16[3840,2048]{1,0:T(8,128)(2,1)} %gather_fusion, pred[3840]{0:T(1024)(128)(4,1)S(1)} %get-tuple-element.5, pred[3840]{0:T(1024)(128)(4,1)S(1)} %get-tuple-element.4), kind=kOutput, calls=%fused_computation.14 | convolution fusion | flops 4043243520 | bytes 18750976 | tf_op jit(solution)/shard_map/dot_general | solution.py:85
  460.8 0.0 reduce-scatter.5.cloned.1.call-update
  460.8 0.6 dynamic_slice.14
  461.4 0.6 dynamic_slice.15
  462.1 31.9 %reduce-scatter.5.cloned.1.call-done = bf16[480,256]{1,0:T(8,128)(2,1)} async-done(((bf16[3840,256]{1,0:T(8,128)(2,1)}), bf16[480,256]{1,0:T(8,128)(2,1)}) %reduce-scatter.5.cloned.1.call-update) | async-done | bytes 245776 | tf_op jit(solution)/shard_map/reduce_scatter | solution.py:84
  494.0 1.7 all_to_all.14
  495.7 6.9 %all-to-all-start = ((bf16[16,30,256]{2,1,0:T(8,128)(2,1)}), bf16[16,30,256]{2,1,0:T(8,128)(2,1)S(1)}, u32[]{:S(2)}, u32[]{:S(2)}) async-start(bf16[16,30,256]{2,1,0:T(8,128)(2,1)} %all_to_all.14), calls=%async_computation.2 | async-start | bytes 524288 | tf_op jit(solution)/shard_map/all_to_all | solution.py:90
  502.6 1.3 fusion.27
  503.9 0.6 compare_select_fusion.1
  504.6 6.5 %all-to-all-done = bf16[16,30,256]{2,1,0:T(8,128)(2,1)S(1)} async-done(((bf16[16,30,256]{2,1,0:T(8,128)(2,1)}), bf16[16,30,256]{2,1,0:T(8,128)(2,1)S(1)}, u32[]{:S(2)}, u32[]{:S(2)}) %all-to-all-start) | async-done | bytes 245792 | tf_op jit(solution)/shard_map/all_to_all | solution.py:90
  511.1 0.1 copy.14
  511.3 0.1 copy.15
  511.4 4.4 gather_fusion.1
  515.7 5.3 select_select_fusion
  (10 shorter events, 0.1 us)
Async XLA Ops:
  7.2 443.7 %copy-start = (bf16[4,512,256]{2,1,0:T(8,128)(2,1)S(1)}, bf16[4,512,256]{2,1,0:T(8,128)(2,1)}, u32[]{:S(2)}) copy-start(bf16[4,512,256]{2,1,0:T(8,128)(2,1)} %param.17) | copy-start | bytes 3145732
  7.2 76.3 %all-gather.5.cloned.1.call-start = ((), (), s32[]{:S(2)}) async-start(), calls=%async_computation.3 | async-start | bytes 8912896 | tf_op jit(solution)/shard_map/all_gather | solution.py:36
  7.9 148.2 %all-gather.7.cloned.1.call-start = ((), (), s32[]{:S(2)}) async-start(), calls=%async_computation.4 | async-start | bytes 8912896 | tf_op jit(solution)/shard_map/all_gather | solution.py:41
  8.7 220.1 %all-gather.9.cloned.1.call-start = ((), (), s32[]{:S(2)}) async-start(), calls=%async_computation.5 | async-start | bytes 8912896 | tf_op jit(solution)/shard_map/all_gather | solution.py:47
  9.4 294.9 %reduce-scatter.3.cloned.1.call-start = ((), (), s32[]{:S(2)}) async-start(), calls=%async_computation.6 | async-start | bytes 8847360 | tf_op jit(solution)/shard_map/reduce_scatter | solution.py:52
  9.4 5.5 %copy-start.1 = (bf16[960,4096]{1,0:T(8,128)(2,1)S(1)}, bf16[960,4096]{1,0:T(8,128)(2,1)}, u32[]{:S(2)}) copy-start(bf16[960,4096]{1,0:T(8,128)(2,1)} %param.10) | copy-start | bytes 23592964
  9.5 74.1 %copy-start.4 = (f32[4096]{0:T(1024)S(1)}, f32[4096]{0:T(1024)}, u32[]{:S(2)}) copy-start(f32[4096]{0:T(1024)} %param.12) | copy-start | bytes 49156
  9.5 74.1 %copy-start.5 = (f32[4096]{0:T(1024)S(1)}, f32[4096]{0:T(1024)}, u32[]{:S(2)}) copy-start(f32[4096]{0:T(1024)} %param.11) | copy-start | bytes 49156
  254.6 159.3 %all-gather.11.cloned.1.call-start = ((), (), s32[]{:S(2)}) async-start(), calls=%async_computation.7 | async-start | bytes 16711680 | tf_op jit(solution)/shard_map/all_gather | solution.py:81
  254.7 53.4 %copy-start.3 = (s32[3840]{0:T(1024)S(1)}, s32[3840]{0:T(1024)}, u32[]{:S(2)}) copy-start(s32[3840]{0:T(1024)} %param.19) | copy-start | bytes 46084
  306.5 144.4 %copy-start.2 = (bf16[960,512]{1,0:T(8,128)(2,1)}, bf16[960,512]{1,0:T(8,128)(2,1)S(1)}, u32[]{:S(2)}) copy-start(bf16[960,512]{1,0:T(8,128)(2,1)S(1)} %add_convert_fusion.1) | copy-start | bytes 2949124
  308.0 186.0 %reduce-scatter.5.cloned.1.call-start = ((), (), s32[]{:S(2)}) async-start(), calls=%async_computation.8 | async-start | bytes 2211840 | tf_op jit(solution)/shard_map/reduce_scatter | solution.py:84
  495.7 15.4 %all-to-all-start = ((bf16[16,30,256]{2,1,0:T(8,128)(2,1)}), bf16[16,30,256]{2,1,0:T(8,128)(2,1)S(1)}, u32[]{:S(2)}, u32[]{:S(2)}) async-start(bf16[16,30,256]{2,1,0:T(8,128)(2,1)} %all_to_all.14), calls=%async_computation.2 | async-start | bytes 524288 | tf_op jit(solution)/shard_map/all_to_all | solution.py:90
Sparse Core Ops, SparseCore 0:
  10.2 73.3 all-gather.4
  85.7 70.4 all-gather.6
  158.3 70.4 all-gather.8
  254.7 49.5 reduce-scatter.2
  308.2 105.6 all-gather.10
  460.9 33.0 reduce-scatter.4
where the time goes:
time: 528 us
  waiting for transfers between devices  362 us (69%)
  local copies, waits for them, and re-layouts  62.5 us (12%)
  matrix products  50.1 us (9%)
  other arithmetic  32.3 us (6%)
  between operations  14.3 us (3%)
  starting transfers between devices  7.14 us (1%)
    all_gather x1, waiting for transfers between devices, shards(): every_row = lax.all_gather(merged, 'req', axis=0, tiled=True)  86.2 us
    all_gather x1, waiting for transfers between devices, shards(): lax.all_gather(down_weight, 'req', axis=1, tiled=True)  72.6 us
    all_gather x1, waiting for transfers between devices, shards(): lax.all_gather(gate_weight, 'req', axis=1, tiled=True)  66.4 us
    all_gather x1, waiting for transfers between devices, shards(): lax.all_gather(up_weight, 'req', axis=1, tiled=True)  58.2 us
    reduce_scatter x1, waiting for transfers between devices, shards(): lax.psum_scatter(partial_value.astype(jnp.bfloat16), 'mlp', scatter_dimen...  37.6 us
    gather x1, local copies, waits for them, and re-layouts, shards(): picked_rows = jnp.take(every_row, jnp.maximum(sources, 0), axis=0)  37 us
    reduce_scatter x1, waiting for transfers between devices, shards(): lax.psum_scatter(jnp.dot(picked_rows, weight_cols, preferred_element_type...  31.9 us
    dot_general x1, matrix products, shards(): lax.dot_general(hidden, lax.all_gather(down_weight, 'req', axis=1, tiled=...  25.9 us
  transfers between devices with their start and end apart: 7, of which 7 were waited for; matrix products, arithmetic and copies ran while one was open for 11% of the time, Pallas kernels for 0%

commit v1 on v0

--- a/solution.py
+++ b/solution.py
@@ -78,7 +78,21 @@
         .at[rows_at]
         .set(jnp.arange(slot_count, dtype=jnp.int32), mode="drop")
     )
-    every_row = lax.all_gather(merged, "req", axis=0, tiled=True)
+    ways, here, hop = (lax.axis_size("req"), lax.axis_index("req"), merged.shape[0])
+    dims = [n * ways if d == 0 else n for d, n in enumerate(merged.shape)]
+    full = lax.dynamic_update_slice_in_dim(
+        jnp.zeros(dims, merged.dtype), merged, here * hop, axis=0
+    )
+    going_up = going_down = merged
+    for far in range(1, ways // 2 + 1):
+        going_up = lax.ppermute(going_up, "req", [(d, (d + 1) % ways) for d in range(ways)])
+        full = lax.dynamic_update_slice_in_dim(full, going_up, (here - far) % ways * hop, axis=0)
+        if 2 * far < ways:
+            going_down = lax.ppermute(going_down, "req", [(d, (d - 1) % ways) for d in range(ways)])
+            full = lax.dynamic_update_slice_in_dim(
+                full, going_down, (here + far) % ways * hop, axis=0
+            )
+    every_row = full
     picked_rows = jnp.take(every_row, jnp.maximum(sources, 0), axis=0)
     picked_rows = jnp.where(sources[:, None] >= 0, picked_rows, jnp.zeros_like(picked_rows))
     summed = lax.psum_scatter(

time: 528 us -> 621 us (1.18)
  starting transfers between devices: 7.14 us -> 46.1 us
  local copies, waits for them, and re-layouts: 62.5 us -> 96.7 us
  waiting for transfers between devices: 362 us -> 377 us
    ppermute x0 -> x15, waiting for transfers between devices: none -> 98.8 us  [the longest x8 68 us: shards(): lax.ppermute(going_up, 'req', [(d, (d + 1) % ways) for d in range(ways)])]
    all_gather x1 -> x0, waiting for transfers between devices: 86.2 us -> none  [shards(): every_row = lax.all_gather(merged, 'req', axis=0, tiled=True)]
    ppermute x0 -> x15, starting transfers between devices: none -> 38.9 us  [the longest x7 37.2 us: shards(): lax.ppermute(going_down, 'req', [(d, (d - 1) % ways) for d in range(ways)])]
    dynamic_update_slice x0 -> x16, local copies, waits for them, and re-layouts: none -> 27.6 us  [the longest x8 14.5 us: shards(): lax.dynamic_update_slice_in_dim(full, going_up, (here - far) % ways * hop...]
    another operation x0 -> x1, local copies, waits for them, and re-layouts: none -> 7.5 us
  transfers between devices with their start and end apart: 7 -> 21, of which waited for: 7 -> 15; matrix products, arithmetic and copies ran while one was open for 11% -> 15% of each run, Pallas kernels for 0% -> 0%
where the time goes in v1:
time: 621 us; the launch traced here: 620 us
  waiting for transfers between devices  377 us (61%)
  local copies, waits for them, and re-layouts  96.7 us (16%)
  matrix products  50.1 us (8%)
  starting transfers between devices  46.1 us (7%)
  other arithmetic  35.3 us (6%)
  between operations  14.3 us (2%)
    all_gather x1, waiting for transfers between devices, shards(): lax.all_gather(down_weight, 'req', axis=1, tiled=True)  72.6 us
    ppermute x8, waiting for transfers between devices, shards(): lax.ppermute(going_up, 'req', [(d, (d + 1) % ways) for d in range(ways)])  68 us
    all_gather x1, waiting for transfers between devices, shards(): lax.all_gather(gate_weight, 'req', axis=1, tiled=True)  64.3 us
    all_gather x1, waiting for transfers between devices, shards(): lax.all_gather(up_weight, 'req', axis=1, tiled=True)  58.2 us
    reduce_scatter x1, waiting for transfers between devices, shards(): lax.psum_scatter(partial_value.astype(jnp.bfloat16), 'mlp', scatter_dimen...  37.6 us
    reduce_scatter x1, waiting for transfers between devices, shards(): lax.psum_scatter(jnp.dot(picked_rows, weight_cols, preferred_element_type...  37.4 us
    ppermute x7, starting transfers between devices, shards(): lax.ppermute(going_down, 'req', [(d, (d - 1) % ways) for d in range(ways)])  37.2 us
    gather x1, local copies, waits for them, and re-layouts, shards(): picked_rows = jnp.take(every_row, jnp.maximum(sources, 0), axis=0)  37 us
  transfers between devices with their start and end apart: 21, of which 15 were waited for; matrix products, arithmetic and copies ran while one was open for 15% of the time, Pallas kernels for 0%

profile of v1, /device:TPU:0, one launch (start us, length us, event | category | flops | bytes accessed | tf_op | source)
XLA Modules:
  0.0 619.8 jit_solution(3724162003459512692)
XLA Ops:
  7.2 0.7 all-gather.4.cloned.1.call-update
  8.0 0.7 all-gather.6.cloned.1.call-update
  8.7 0.7 all-gather.8.cloned.1.call-update
  9.5 4.3 convert_reduce_fusion
  13.8 5.4 multiply_reduce_fusion
  19.2 64.3 %all-gather.4.cloned.1.call-done = bf16[4096,1024]{0,1:T(8,128)(2,1)} async-done(((bf16[4096,64]{0,1:T(8,128)(2,1)}), bf16[4096,1024]{0,1:T(8,128)(2,1)}) %all-gather.4.cloned.1.call-update) | async-done | bytes 8388624 | tf_op jit(solution)/shard_map/all_gather | solution.py:36
  83.5 14.4 %fusion.31 = f32[960,1024]{1,0:T(8,128)} fusion(bf16[4096,1024]{0,1:T(8,128)(2,1)} %all-gather.4.cloned.1.call-done, bf16[960,4096]{1,0:T(8,128)(2,1)} %param.10, f32[4096]{0:T(1024)S(1)} %copy-done.6, f32[4096]{0:T(1024)S(1)} %copy-done.7, f32[960]{0:T(1024)S(1)} %add_rsqrt_fusion, f32[960]{0:T(1024)S(1)} %broadcast_multiply_fusion), kind=kOutput, calls=%fused_computation.84 | convolution fusion | flops 8076656640 | bytes 20225536 | tf_op jit(solution)/shard_map/dot_general | solution.py:34
  97.9 58.2 %all-gather.6.cloned.1.call-done = bf16[4096,1024]{0,1:T(8,128)(2,1)} async-done(((bf16[4096,64]{0,1:T(8,128)(2,1)}), bf16[4096,1024]{0,1:T(8,128)(2,1)}) %all-gather.6.cloned.1.call-update) | async-done | bytes 8388624 | tf_op jit(solution)/shard_map/all_gather | solution.py:41
  156.1 72.6 %all-gather.8.cloned.1.call-done = bf16[4096,1024]{0,1:T(8,128)(2,1)} async-done(((bf16[4096,64]{0,1:T(8,128)(2,1)}), bf16[4096,1024]{0,1:T(8,128)(2,1)}) %all-gather.8.cloned.1.call-update) | async-done | bytes 8388624 | tf_op jit(solution)/shard_map/all_gather | solution.py:47
  228.8 25.9 %convolution_convert_fusion = bf16[960,4096]{1,0:T(8,128)(2,1)} fusion(bf16[4096,1024]{0,1:T(8,128)(2,1)} %all-gather.8.cloned.1.call-done, f32[960,1024]{1,0:T(8,128)} %fusion.31, bf16[4096,1024]{0,1:T(8,128)(2,1)} %all-gather.6.cloned.1.call-done, bf16[960,4096]{1,0:T(8,128)(2,1)} %param.10, f32[4096]{0:T(1024)S(1)} %copy-done.6, f32[4096]{0:T(1024)S(1)} %copy-done.7, ...), kind=kOutput, calls=%fused_computation.13 | convolution fusion | flops 16139550720 | bytes 36478464 | tf_op jit(solution)/shard_map/dot_general | solution.py:45
  254.7 11.3 %convert_element_type.26 = f32[960,4096]{1,0:T(8,128)} convert(bf16[960,4096]{1,0:T(8,128)(2,1)} %param.10) | non-fusion elementwise | flops 3932160 | bytes 23592960 | tf_op jit(solution)/shard_map/convert_element_type | solution.py:32
  266.0 0.8 dynamic_slice.13
  266.8 37.6 %reduce-scatter.3.cloned.1.call-done = bf16[960,512]{1,0:T(8,128)(2,1)} async-done(((bf16[960,4096]{1,0:T(8,128)(2,1)}), bf16[960,512]{1,0:T(8,128)(2,1)}) %reduce-scatter.3.cloned.1.call-update) | async-done | bytes 983056 | tf_op jit(solution)/shard_map/reduce_scatter | solution.py:52
  304.3 2.2 add_convert_fusion.1
  307.1 1.6 collective-permute-start
  308.7 3.8 collective-permute-start.1
  312.5 20.9 %collective-permute-done = bf16[240,2048]{1,0:T(8,128)(2,1)S(1)} collective-permute-done((bf16[240,2048]{1,0:T(8,128)(2,1)S(1)}, bf16[240,2048]{1,0:T(8,128)(2,1)S(1)}, u32[]{:S(2)}, u32[]{:S(2)}) %collective-permute-start) | collective-permute-done | bytes 983072 | tf_op jit(solution)/shard_map/ppermute | solution.py:88
  333.5 5.3 collective-permute-start.3
  338.8 20.0 %collective-permute-done.2 = bf16[240,2048]{1,0:T(8,128)(2,1)S(1)} collective-permute-done((bf16[240,2048]{1,0:T(8,128)(2,1)S(1)}, bf16[240,2048]{1,0:T(8,128)(2,1)S(1)}, u32[]{:S(2)}, u32[]{:S(2)}) %collective-permute-start.2) | collective-permute-done | bytes 983072 | tf_op jit(solution)/shard_map/ppermute | solution.py:88
  358.8 1.0 copy-done.2
  359.8 5.3 collective-permute-start.5
  365.1 19.2 %collective-permute-done.4 = bf16[240,2048]{1,0:T(8,128)(2,1)} collective-permute-done((bf16[240,2048]{1,0:T(8,128)(2,1)S(1)}, bf16[240,2048]{1,0:T(8,128)(2,1)}, u32[]{:S(2)}, u32[]{:S(2)}) %collective-permute-start.4) | collective-permute-done | bytes 983072 | tf_op jit(solution)/shard_map/ppermute | solution.py:88
  384.4 2.3 select_reduce_fusion.1
  386.6 2.4 convert_reduce_fusion.1
  389.1 14.6 %scatter_custom_fusion = s32[3840]{0:T(1024)S(1)} fusion(s32[3840]{0:T(1024)S(1)} %compare_select_fusion, s32[3840]{0:T(1024)S(1)} %iota.16, s32[]{:T(128)} %constant.186.clone.1), kind=kCustom, calls=%fused_computation.51 | custom fusion | bytes 15364 | tf_op jit(solution)/shard_map/scatter | solution.py:79
  403.7 5.4 collective-permute-start.7
  409.5 7.5 %broadcast.140 = bf16[3840,2048]{1,0:T(8,128)(2,1)} broadcast(bf16[]{:T(256)} %constant.199.clone.1), dimensions={} | broadcast | bytes 15728642 | tf_op jit(solution)/shard_map/broadcast.7
  417.0 1.0 constant_dynamic-update-slice_fusion.15
  418.0 2.3 constant_dynamic-update-slice_fusion.14
  420.3 6.5 %collective-permute-done.7 = bf16[240,2048]{1,0:T(8,128)(2,1)} collective-permute-done((bf16[240,2048]{1,0:T(8,128)(2,1)}, bf16[240,2048]{1,0:T(8,128)(2,1)}, u32[]{:S(2)}, u32[]{:S(2)}) %collective-permute-start.7) | collective-permute-done | bytes 983072 | tf_op jit(solution)/shard_map/ppermute | solution.py:91
  426.8 5.8 collective-permute-start.9
  432.6 2.3 constant_dynamic-update-slice_fusion.13
  434.9 2.3 constant_dynamic-update-slice_fusion.12
  437.2 2.3 constant_dynamic-update-slice_fusion.11
  439.4 2.3 constant_dynamic-update-slice_fusion.10
  441.7 7.7 %collective-permute-done.9 = bf16[240,2048]{1,0:T(8,128)(2,1)S(1)} collective-permute-done((bf16[240,2048]{1,0:T(8,128)(2,1)}, bf16[240,2048]{1,0:T(8,128)(2,1)S(1)}, u32[]{:S(2)}, u32[]{:S(2)}) %collective-permute-start.9) | collective-permute-done | bytes 983072 | tf_op jit(solution)/shard_map/ppermute | solution.py:91
  449.4 5.7 collective-permute-start.11
  455.1 2.3 constant_dynamic-update-slice_fusion.9
  457.4 2.3 constant_dynamic-update-slice_fusion.8
  459.7 2.2 constant_dynamic-update-slice_fusion.7
  461.9 2.2 constant_dynamic-update-slice_fusion.6
  464.2 7.1 %collective-permute-done.11 = bf16[240,2048]{1,0:T(8,128)(2,1)S(1)} collective-permute-done((bf16[240,2048]{1,0:T(8,128)(2,1)S(1)}, bf16[240,2048]{1,0:T(8,128)(2,1)S(1)}, u32[]{:S(2)}, u32[]{:S(2)}) %collective-permute-start.11) | collective-permute-done | bytes 983072 | tf_op jit(solution)/shard_map/ppermute | solution.py:91
  471.2 5.8 collective-permute-start.13
  477.1 1.1 constant_dynamic-update-slice_fusion.5
  478.1 1.2 collective-permute-done.12
  479.3 1.0 constant_dynamic-update-slice_fusion.4
  480.3 1.0 constant_dynamic-update-slice_fusion.3
  481.4 1.0 constant_dynamic-update-slice_fusion.2
  482.4 9.4 %collective-permute-done.13 = bf16[240,2048]{1,0:T(8,128)(2,1)S(1)} collective-permute-done((bf16[240,2048]{1,0:T(8,128)(2,1)S(1)}, bf16[240,2048]{1,0:T(8,128)(2,1)S(1)}, u32[]{:S(2)}, u32[]{:S(2)}) %collective-permute-start.13) | collective-permute-done | bytes 983072 | tf_op jit(solution)/shard_map/ppermute | solution.py:91
  491.8 1.0 constant_dynamic-update-slice_fusion.1
  492.8 6.8 %collective-permute-done.14 = bf16[240,2048]{1,0:T(8,128)(2,1)S(1)} collective-permute-done((bf16[240,2048]{1,0:T(8,128)(2,1)S(1)}, bf16[240,2048]{1,0:T(8,128)(2,1)S(1)}, u32[]{:S(2)}, u32[]{:S(2)}) %collective-permute-start.14) | collective-permute-done | bytes 983072 | tf_op jit(solution)/shard_map/ppermute | solution.py:88
  499.6 1.1 constant_dynamic-update-slice_fusion
  500.6 37.0 %gather_fusion = bf16[3840,2048]{1,0:T(8,128)(2,1)} fusion(bf16[3840,2048]{1,0:T(8,128)(2,1)} %constant_dynamic-update-slice_fusion, s32[4096]{0:T(1024)S(1)} %pad_clamp_fusion), kind=kCustom, calls=%fused_computation | custom fusion | bytes 31472640 | tf_op jit(solution)/shard_map/jit(_take)/gather | solution.py:96
  537.6 9.9 %fusion.7 = bf16[3840,256]{1,0:T(8,128)(2,1)} fusion(bf16[2048,256]{1,0:T(8,128)(2,1)S(1)} %bitcast.12, bf16[3840,2048]{1,0:T(8,128)(2,1)} %gather_fusion, pred[3840]{0:T(1024)(128)(4,1)S(1)} %get-tuple-element.5, pred[3840]{0:T(1024)(128)(4,1)S(1)} %get-tuple-element.4), kind=kOutput, calls=%fused_computation.14 | convolution fusion | flops 4043243520 | bytes 18750976 | tf_op jit(solution)/shard_map/dot_general | solution.py:99
  547.5 0.7 dynamic_slice.14
  548.2 0.6 dynamic_slice.15
  548.8 37.4 %reduce-scatter.5.cloned.1.call-done = bf16[480,256]{1,0:T(8,128)(2,1)} async-done(((bf16[3840,256]{1,0:T(8,128)(2,1)}), bf16[480,256]{1,0:T(8,128)(2,1)}) %reduce-scatter.5.cloned.1.call-update) | async-done | bytes 245776 | tf_op jit(solution)/shard_map/reduce_scatter | solution.py:98
  586.3 1.7 all_to_all.14
  588.0 6.9 %all-to-all-start = ((bf16[16,30,256]{2,1,0:T(8,128)(2,1)}), bf16[16,30,256]{2,1,0:T(8,128)(2,1)S(1)}, u32[]{:S(2)}, u32[]{:S(2)}) async-start(bf16[16,30,256]{2,1,0:T(8,128)(2,1)} %all_to_all.14), calls=%async_computation.2 | async-start | bytes 524288 | tf_op jit(solution)/shard_map/all_to_all | solution.py:104
  594.9 1.4 fusion.27
  596.3 0.7 compare_select_fusion.1
  597.0 6.4 %all-to-all-done = bf16[16,30,256]{2,1,0:T(8,128)(2,1)S(1)} async-done(((bf16[16,30,256]{2,1,0:T(8,128)(2,1)}), bf16[16,30,256]{2,1,0:T(8,128)(2,1)S(1)}, u32[]{:S(2)}, u32[]{:S(2)}) %all-to-all-start) | async-done | bytes 245792 | tf_op jit(solution)/shard_map/all_to_all | solution.py:104
  603.7 4.4 gather_fusion.1
  608.0 5.3 select_select_fusion
  (48 shorter events, 1.3 us)
Async XLA Ops:
  7.2 530.4 %copy-start = (bf16[4,512,256]{2,1,0:T(8,128)(2,1)S(1)}, bf16[4,512,256]{2,1,0:T(8,128)(2,1)}, u32[]{:S(2)}) copy-start(bf16[4,512,256]{2,1,0:T(8,128)(2,1)} %param.17) | copy-start | bytes 3145732
  7.2 76.4 %copy-start.7 = (f32[4096]{0:T(1024)S(1)}, f32[4096]{0:T(1024)}, u32[]{:S(2)}) copy-start(f32[4096]{0:T(1024)} %param.11) | copy-start | bytes 49156
  7.2 76.3 %copy-start.6 = (f32[4096]{0:T(1024)S(1)}, f32[4096]{0:T(1024)}, u32[]{:S(2)}) copy-start(f32[4096]{0:T(1024)} %param.12) | copy-start | bytes 49156
  7.2 76.3 %all-gather.4.cloned.1.call-start = ((), (), s32[]{:S(2)}) async-start(), calls=%async_computation.3 | async-start | bytes 8912896 | tf_op jit(solution)/shard_map/all_gather | solution.py:36
  7.9 148.2 %all-gather.6.cloned.1.call-start = ((), (), s32[]{:S(2)}) async-start(), calls=%async_computation.4 | async-start | bytes 8912896 | tf_op jit(solution)/shard_map/all_gather | solution.py:41
  8.7 220.1 %all-gather.8.cloned.1.call-start = ((), (), s32[]{:S(2)}) async-start(), calls=%async_computation.5 | async-start | bytes 8912896 | tf_op jit(solution)/shard_map/all_gather | solution.py:47
  9.4 294.9 %reduce-scatter.3.cloned.1.call-start = ((), (), s32[]{:S(2)}) async-start(), calls=%async_computation.6 | async-start | bytes 8847360 | tf_op jit(solution)/shard_map/reduce_scatter | solution.py:52
  254.6 129.7 %copy-start.5 = (s32[3840]{0:T(1024)S(1)}, s32[3840]{0:T(1024)}, u32[]{:S(2)}) copy-start(s32[3840]{0:T(1024)} %param.19) | copy-start | bytes 46084
  254.6 331.6 %reduce-scatter.5.cloned.1.call-start = ((), (), s32[]{:S(2)}) async-start(), calls=%async_computation.7 | async-start | bytes 2211840 | tf_op jit(solution)/shard_map/reduce_scatter | solution.py:98
  306.5 150.9 %copy-start.1 = (bf16[960,512]{1,0:T(8,128)(2,1)}, bf16[960,512]{1,0:T(8,128)(2,1)S(1)}, u32[]{:S(2)}) copy-start(bf16[960,512]{1,0:T(8,128)(2,1)S(1)} %add_convert_fusion.1) | copy-start | bytes 2949124
  307.1 26.3 %collective-permute-start = (bf16[240,2048]{1,0:T(8,128)(2,1)S(1)}, bf16[240,2048]{1,0:T(8,128)(2,1)S(1)}, u32[]{:S(2)}, u32[]{:S(2)}) collective-permute-start(bf16[240,2048]{1,0:T(8,128)(2,1)S(1)} %reshape.67), channel_id=1, source_target_pairs={{0,8},{8,16},{16,24},{24,32},{32,40},{40,48},{48,56},{56,64},{64,7... | collective-permute-start | bytes 2949128 | tf_op jit(solution)/shard_map/ppermute | solution.py:88
  308.7 24.7 %collective-permute-start.1 = (bf16[240,2048]{1,0:T(8,128)(2,1)S(1)}, bf16[240,2048]{1,0:T(8,128)(2,1)S(1)}, u32[]{:S(2)}, u32[]{:S(2)}) collective-permute-start(bf16[240,2048]{1,0:T(8,128)(2,1)S(1)} %reshape.67), channel_id=1, source_target_pairs={{0,120},{8,0},{16,8},{24,16},{32,24},{40,32},{48,40},{56,48},{64,5... | collective-permute-start | bytes 2949128 | tf_op jit(solution)/shard_map/ppermute | solution.py:91
  333.4 50.8 %copy-start.4 = (bf16[240,2048]{1,0:T(8,128)(2,1)}, bf16[240,2048]{1,0:T(8,128)(2,1)S(1)}, u32[]{:S(2)}) copy-start(bf16[240,2048]{1,0:T(8,128)(2,1)S(1)} %collective-permute-done) | copy-start | bytes 2949124
  333.4 25.3 %collective-permute-start.2 = (bf16[240,2048]{1,0:T(8,128)(2,1)S(1)}, bf16[240,2048]{1,0:T(8,128)(2,1)S(1)}, u32[]{:S(2)}, u32[]{:S(2)}) collective-permute-start(bf16[240,2048]{1,0:T(8,128)(2,1)S(1)} %collective-permute-done), channel_id=1, source_target_pairs={{0,8},{8,16},{16,24},{24,32},{32,40},{40,48},{48,56},{56,64},{64,7... | collective-permute-start | bytes 2949128 | tf_op jit(solution)/shard_map/ppermute | solution.py:88
  333.4 50.8 %copy-start.3 = (bf16[240,2048]{1,0:T(8,128)(2,1)}, bf16[240,2048]{1,0:T(8,128)(2,1)S(1)}, u32[]{:S(2)}) copy-start(bf16[240,2048]{1,0:T(8,128)(2,1)S(1)} %collective-permute-done.1) | copy-start | bytes 2949124
  333.5 26.3 %collective-permute-start.3 = (bf16[240,2048]{1,0:T(8,128)(2,1)S(1)}, bf16[240,2048]{1,0:T(8,128)(2,1)}, u32[]{:S(2)}, u32[]{:S(2)}) collective-permute-start(bf16[240,2048]{1,0:T(8,128)(2,1)S(1)} %collective-permute-done.1), channel_id=1, source_target_pairs={{0,120},{8,0},{16,8},{24,16},{32,24},{40,32},{48,40},{56,48},{64,5... | collective-permute-start | bytes 2949128 | tf_op jit(solution)/shard_map/ppermute | solution.py:91
  358.8 1.0 copy-start.2
  359.8 24.5 %collective-permute-start.4 = (bf16[240,2048]{1,0:T(8,128)(2,1)S(1)}, bf16[240,2048]{1,0:T(8,128)(2,1)}, u32[]{:S(2)}, u32[]{:S(2)}) collective-permute-start(bf16[240,2048]{1,0:T(8,128)(2,1)S(1)} %collective-permute-done.2), channel_id=1, source_target_pairs={{0,8},{8,16},{16,24},{24,32},{32,40},{40,48},{48,56},{56,64},{64,7... | collective-permute-start | bytes 2949128 | tf_op jit(solution)/shard_map/ppermute | solution.py:88
  359.8 43.9 %collective-permute-start.5 = (bf16[240,2048]{1,0:T(8,128)(2,1)}, bf16[240,2048]{1,0:T(8,128)(2,1)}, u32[]{:S(2)}, u32[]{:S(2)}) collective-permute-start(bf16[240,2048]{1,0:T(8,128)(2,1)} %collective-permute-done.3), channel_id=1, source_target_pairs={{0,120},{8,0},{16,8},{24,16},{32,24},{40,32},{48,40},{56,48},{64,5... | collective-permute-start | bytes 2949128 | tf_op jit(solution)/shard_map/ppermute | solution.py:91
  384.3 24.8 %collective-permute-start.6 = (bf16[240,2048]{1,0:T(8,128)(2,1)}, bf16[240,2048]{1,0:T(8,128)(2,1)}, u32[]{:S(2)}, u32[]{:S(2)}) collective-permute-start(bf16[240,2048]{1,0:T(8,128)(2,1)} %collective-permute-done.4), channel_id=1, source_target_pairs={{0,8},{8,16},{16,24},{24,32},{32,40},{40,48},{48,56},{56,64},{64,7... | collective-permute-start | bytes 2949128 | tf_op jit(solution)/shard_map/ppermute | solution.py:88
  403.7 23.1 %collective-permute-start.7 = (bf16[240,2048]{1,0:T(8,128)(2,1)}, bf16[240,2048]{1,0:T(8,128)(2,1)}, u32[]{:S(2)}, u32[]{:S(2)}) collective-permute-start(bf16[240,2048]{1,0:T(8,128)(2,1)} %collective-permute-done.5), channel_id=1, source_target_pairs={{0,120},{8,0},{16,8},{24,16},{32,24},{40,32},{48,40},{56,48},{64,5... | collective-permute-start | bytes 2949128 | tf_op jit(solution)/shard_map/ppermute | solution.py:91
  409.1 25.8 %collective-permute-start.8 = (bf16[240,2048]{1,0:T(8,128)(2,1)}, bf16[240,2048]{1,0:T(8,128)(2,1)}, u32[]{:S(2)}, u32[]{:S(2)}) collective-permute-start(bf16[240,2048]{1,0:T(8,128)(2,1)} %collective-permute-done.6), channel_id=1, source_target_pairs={{0,8},{8,16},{16,24},{24,32},{32,40},{40,48},{48,56},{56,64},{64,7... | collective-permute-start | bytes 2949128 | tf_op jit(solution)/shard_map/ppermute | solution.py:88
  426.8 22.6 %collective-permute-start.9 = (bf16[240,2048]{1,0:T(8,128)(2,1)}, bf16[240,2048]{1,0:T(8,128)(2,1)S(1)}, u32[]{:S(2)}, u32[]{:S(2)}) collective-permute-start(bf16[240,2048]{1,0:T(8,128)(2,1)} %collective-permute-done.7), channel_id=1, source_target_pairs={{0,120},{8,0},{16,8},{24,16},{32,24},{40,32},{48,40},{56,48},{64,5... | collective-permute-start | bytes 2949128 | tf_op jit(solution)/shard_map/ppermute | solution.py:91
  434.9 22.5 %collective-permute-start.10 = (bf16[240,2048]{1,0:T(8,128)(2,1)}, bf16[240,2048]{1,0:T(8,128)(2,1)S(1)}, u32[]{:S(2)}, u32[]{:S(2)}) collective-permute-start(bf16[240,2048]{1,0:T(8,128)(2,1)} %collective-permute-done.8), channel_id=1, source_target_pairs={{0,8},{8,16},{16,24},{24,32},{32,40},{40,48},{48,56},{56,64},{64,7... | collective-permute-start | bytes 2949128 | tf_op jit(solution)/shard_map/ppermute | solution.py:88
  449.4 21.8 %collective-permute-start.11 = (bf16[240,2048]{1,0:T(8,128)(2,1)S(1)}, bf16[240,2048]{1,0:T(8,128)(2,1)S(1)}, u32[]{:S(2)}, u32[]{:S(2)}) collective-permute-start(bf16[240,2048]{1,0:T(8,128)(2,1)S(1)} %collective-permute-done.9), channel_id=1, source_target_pairs={{0,120},{8,0},{16,8},{24,16},{32,24},{40,32},{48,40},{56,48},{64,5... | collective-permute-start | bytes 2949128 | tf_op jit(solution)/shard_map/ppermute | solution.py:91
  457.4 21.9 %collective-permute-start.12 = (bf16[240,2048]{1,0:T(8,128)(2,1)S(1)}, bf16[240,2048]{1,0:T(8,128)(2,1)S(1)}, u32[]{:S(2)}, u32[]{:S(2)}) collective-permute-start(bf16[240,2048]{1,0:T(8,128)(2,1)S(1)} %collective-permute-done.10), channel_id=1, source_target_pairs={{0,8},{8,16},{16,24},{24,32},{32,40},{40,48},{48,56},{56,64},{64,7... | collective-permute-start | bytes 2949128 | tf_op jit(solution)/shard_map/ppermute | solution.py:88
  471.2 20.5 %collective-permute-start.13 = (bf16[240,2048]{1,0:T(8,128)(2,1)S(1)}, bf16[240,2048]{1,0:T(8,128)(2,1)S(1)}, u32[]{:S(2)}, u32[]{:S(2)}) collective-permute-start(bf16[240,2048]{1,0:T(8,128)(2,1)S(1)} %collective-permute-done.11), channel_id=1, source_target_pairs={{0,120},{8,0},{16,8},{24,16},{32,24},{40,32},{48,40},{56,48},{64,5... | collective-permute-start | bytes 2949128 | tf_op jit(solution)/shard_map/ppermute | solution.py:91
  479.3 20.2 %collective-permute-start.14 = (bf16[240,2048]{1,0:T(8,128)(2,1)S(1)}, bf16[240,2048]{1,0:T(8,128)(2,1)S(1)}, u32[]{:S(2)}, u32[]{:S(2)}) collective-permute-start(bf16[240,2048]{1,0:T(8,128)(2,1)S(1)} %collective-permute-done.12), channel_id=1, source_target_pairs={{0,8},{8,16},{16,24},{24,32},{32,40},{40,48},{48,56},{56,64},{64,7... | collective-permute-start | bytes 2949128 | tf_op jit(solution)/shard_map/ppermute | solution.py:88
  588.0 15.4 %all-to-all-start = ((bf16[16,30,256]{2,1,0:T(8,128)(2,1)}), bf16[16,30,256]{2,1,0:T(8,128)(2,1)S(1)}, u32[]{:S(2)}, u32[]{:S(2)}) async-start(bf16[16,30,256]{2,1,0:T(8,128)(2,1)} %all_to_all.14), calls=%async_computation.2 | async-start | bytes 524288 | tf_op jit(solution)/shard_map/all_to_all | solution.py:104
Sparse Core Ops, SparseCore 0:
  10.2 73.3 all-gather.3
  85.7 70.4 all-gather.5
  158.3 70.4 all-gather.7
  254.8 49.5 reduce-scatter.2
  547.7 38.5 reduce-scatter.4
